TPU v7x, 256 devices: a whole 4x4x8 slice. The times are simulated.
256 devices in a mesh: loop: 16 (over y, x), dp: 16 (over z, core).
Axes of the slice: x: 4, y: 4, z: 8, core: 2. Of those that a mesh axis runs over, the one named last changes fastest.
Arguments:
- tokens: bfloat16 [3584, 8192], P('dp', 'loop'), may hold values from -8 to 8
- weight: bfloat16 [8192, 14336], P('loop', 'dp'), as said below
- rounding: float32 [8192, 14336], P('loop', 'dp'), may hold values from -6 to 6
- floor_codes: int32 [8192, 14336], P('loop', 'dp'), may hold values from -1 to 15
- scale_codes: int32 [14336], P('dp'), may hold values from 12 to 15
- zero_codes: int32 [14336], P('dp'), may hold values from 0 to 15
- block_mask: int32 [128, 224], P('loop', 'dp'), may hold values from 0 to 1, as said below
Outputs:
- refined: float32 [8192, 14336], P('loop', 'dp')
Inputs may be any that keep to these rules, and one draw needn't show every extreme that they name: weight equals scales times (floor_codes - zero_point + a fraction in [0, 1)), then is rounded to bfloat16. `block_mask`: the share of surviving blocks differs between column blocks.
All inputs are finite; a program needn't handle non-finite values.
Results may differ from a plain program's by a relative error of at most 0.019.
Values may be sent and summed in bfloat16 or wider, within the bound.
A program may use at most 128 MiB of HBM per device.

v0:
```python
import jax
import jax.numpy as jnp
from jax import lax
from jax.sharding import PartitionSpec as P

BLOCK = 64
ITERS = 2
step_rate = 20.0
reg_weight = 0.05
base_scale = 0.02


def expand(block_mask):
    row_blocks, col_blocks = block_mask.shape
    spread = jnp.broadcast_to(block_mask[:, None, :, None], (row_blocks, BLOCK, col_blocks, BLOCK))
    return spread.reshape(row_blocks * BLOCK, col_blocks * BLOCK).astype(jnp.float32)


def token_product(token_rows, scaled_err):
    return lax.dot_general(
        token_rows, scaled_err, (((0,), (0,)), ((), ())), preferred_element_type=jnp.float32
    )


def per_device(tokens, weight, rounding, floor_codes, scale_codes, zero_codes, block_mask):
    gathered = lax.all_gather(tokens, "dp", axis=0, tiled=True)
    token_count = gathered.shape[0]
    scales = base_scale * jnp.exp2(scale_codes.astype(jnp.float32) * 0.25)
    zero_point = zero_codes.astype(jnp.float32)
    kept_mask = expand(block_mask)
    floors = floor_codes.astype(jnp.float32)
    in_range = ((floor_codes >= 0) & (floor_codes <= 14)).astype(jnp.float32)
    target = weight.astype(jnp.float32)
    for iteration in range(ITERS):
        relaxed = jax.nn.sigmoid(rounding)
        levels = jnp.clip(floors + relaxed, 0.0, 15.0)
        w_delta = (kept_mask * (scales[None, :] * (levels - zero_point[None, :]) - target)).astype(
            jnp.bfloat16
        )
        partial_sum = jnp.dot(gathered, w_delta, preferred_element_type=jnp.float32)
        residual = lax.psum(partial_sum.astype(jnp.bfloat16), "loop").astype(jnp.float32)
        scaled_err = (2.0 / token_count * residual).astype(jnp.bfloat16)
        gradient = token_product(gathered, scaled_err)
        centered = 2.0 * relaxed - 1.0
        descent = gradient * scales[None, :] * in_range - reg_weight * 8.0 * centered**3
        rounding = rounding - step_rate * kept_mask * descent * relaxed * (1.0 - relaxed)
    return rounding


def solution(mesh):
    placed = (
        P("dp", "loop"),
        P("loop", "dp"),
        P("loop", "dp"),
        P("loop", "dp"),
        P("dp"),
        P("dp"),
        P("loop", "dp"),
    )
    return jax.shard_map(
        per_device, mesh=mesh, in_specs=placed, out_specs=P("loop", "dp"), check_vma=False
    )
```

profile of v0, /device:TPU:1, one launch (start us, length us, event | category | flops | bytes accessed | tf_op | source)
XLA Modules:
  0.0 364.3 jit_solution(10741293267602168995)
XLA Ops:
  6.5 0.0 all-gather.2.cloned.1.call-start
  6.5 0.7 all-gather.2.cloned.1.call-update
  7.3 0.0 all-reduce.3.cloned.1.call-start
  7.3 0.7 convert_element_type.50
  8.0 0.1 copy.8
  8.1 2.1 broadcast_in_dim.2
  10.2 4.4 %convert_element_type.51 = f32[512,896]{0,1:T(8,128)} reshape(f32[8,64,14,64]{1,0,3,2:T(8,128)} %broadcast_in_dim.2) | data formatting | bytes 3670016 | tf_op jit(solution)/shard_map/convert_element_type | solution.py:16
  14.6 1.8 copy.9
  16.4 0.0 copy-start.1
  16.4 0.0 copy-start.3
  16.4 2.8 copy.14
  19.2 0.0 copy-done.1
  19.2 1.3 copy.13
  20.5 0.0 copy-done.3
  20.5 0.0 copy-done.4
  20.5 34.1 %all-gather.2.cloned.1.call-done = bf16[3584,512]{1,0:T(8,128)(2,1)} async-done(((bf16[224,512]{1,0:T(8,128)(2,1)}), bf16[3584,512]{1,0:T(8,128)(2,1)}) %all-gather.2.cloned.1.call-update) | async-done | bytes 3670032 | tf_op jit(solution)/shard_map/all_gather | solution.py:26
  54.7 10.1 %fusion.4 = bf16[3584,896]{0,1:T(8,128)(2,1)} fusion(bf16[3584,512]{1,0:T(8,128)(2,1)} %all-gather.2.cloned.1.call-done, f32[512,896]{0,1:T(8,128)} %convert_element_type.51, bf16[512,896]{0,1:T(8,128)(2,1)} %copy.13, s32[512,896]{0,1:T(8,128)S(1)} %copy.9, f32[512,896]{0,1:T(8,128)} %copy.14, f32[896]{0:T(1024)S(1)} %convert_element_type.54, ...), kind=kOutput, calls=%fused_computation.8 | convolution fusion | flops 3297050624 | bytes 16522240 | tf_op jit(solution)/shard_map/dot_general | solution.py:40
  64.7 0.0 all-reduce.3.cloned.1.call-update
  64.8 0.2 all-reduce.5.cloned.1.call-start
  65.0 0.4 compare_and_fusion
  65.4 0.0 copy-start.2
  65.4 131.1 %all-reduce.3.cloned.1.call-done = bf16[3584,896]{0,1:T(8,128)(2,1)} async-done(((bf16[3584,896]{0,1:T(8,128)(2,1)}), bf16[3584,896]{0,1:T(8,128)(2,1)}) %all-reduce.3.cloned.1.call-update) | async-done | bytes 6422544 | tf_op jit(solution)/shard_map/psum | solution.py:41
  196.4 9.5 %fusion.15 = f32[512,896]{0,1:T(8,128)S(1)} fusion(f32[512,896]{0,1:T(8,128)} %copy.14, pred[512,896]{0,1:T(32,128)(4,1)S(1)} %compare_and_fusion, f32[512,896]{0,1:T(8,128)} %convert_element_type.51, bf16[3584,512]{1,0:T(8,128)(2,1)} %all-gather.2.cloned.1.call-done, bf16[3584,896]{0,1:T(8,128)(2,1)} %all-reduce.3.cloned.1.call-done, ...), kind=kOutput, calls=%fused_computation.23 | convolution fusion | flops 3305766912 | bytes 16059904 | tf_op jit(solution)/shard_map/dot_general | solution.py:20
  206.0 0.0 copy-start.6
  206.0 1.2 copy-done.6
  207.2 0.0 copy-done.2
  207.2 0.0 copy-done.5
  207.2 6.2 %fusion.5 = bf16[3584,896]{0,1:T(8,128)(2,1)} fusion(bf16[3584,512]{1,0:T(8,128)(2,1)S(1)} %copy-done.5, f32[512,896]{0,1:T(8,128)S(1)} %copy-done, bf16[512,896]{0,1:T(8,128)(2,1)S(1)} %copy-done.2, s32[512,896]{0,1:T(8,128)S(1)} %copy.9, f32[512,896]{0,1:T(8,128)S(1)} %fusion.15, f32[896]{0:T(1024)S(1)} %convert_element_type.54, ...), kind=kOutput, calls=%fused_computation.9 | convolution fusion | flops 3297050624 | bytes 16522240 | tf_op jit(solution)/shard_map/dot_general | solution.py:40
  213.4 0.0 all-reduce.5.cloned.1.call-update
  213.4 133.4 %all-reduce.5.cloned.1.call-done = bf16[3584,896]{0,1:T(8,128)(2,1)} async-done(((bf16[3584,896]{0,1:T(8,128)(2,1)}), bf16[3584,896]{0,1:T(8,128)(2,1)}) %all-reduce.5.cloned.1.call-update) | async-done | bytes 6422544 | tf_op jit(solution)/shard_map/psum | solution.py:41
  346.7 9.4 %fusion.21 = f32[512,896]{0,1:T(8,128)S(1)} fusion(f32[512,896]{0,1:T(8,128)} %copy-done.6, pred[512,896]{0,1:T(32,128)(4,1)S(1)} %compare_and_fusion, f32[512,896]{0,1:T(8,128)} %convert_element_type.51, bf16[3584,512]{1,0:T(8,128)(2,1)} %all-gather.2.cloned.1.call-done, bf16[3584,896]{0,1:T(8,128)(2,1)} %all-reduce.5.cloned.1.call-done, ...), kind=kOutput, calls=%fused_computation.29 | convolution fusion | flops 3305766912 | bytes 16059904 | tf_op jit(solution)/shard_map/dot_general | solution.py:20
  356.1 1.7 copy.15
  (6 shorter events, 0.0 us)
Async XLA Ops:
  6.5 48.1 %all-gather.2.cloned.1.call-start = ((), (), s32[]{:S(2)}) async-start(), calls=%async_computation | async-start | bytes 3899392 | tf_op jit(solution)/shard_map/all_gather | solution.py:26
  7.3 189.2 %all-reduce.3.cloned.1.call-start = ((), (), s32[]{:S(2)}) async-start(), calls=%async_computation.1 | async-start | bytes 12845056 | tf_op jit(solution)/shard_map/psum | solution.py:41
  16.4 2.8 copy-start.1
  16.4 4.1 %copy-start.3 = (s32[896]{0:T(1024)S(1)}, s32[896]{0:T(1024)}, u32[]{:S(2)}) copy-start(s32[896]{0:T(1024)} %param.12) | copy-start | bytes 10756
  19.2 1.3 copy-start.4
  64.8 282.0 %all-reduce.5.cloned.1.call-start = ((), (), s32[]{:S(2)}) async-start(), calls=%async_computation.2 | async-start | bytes 12845056 | tf_op jit(solution)/shard_map/psum | solution.py:41
  65.4 141.8 %copy-start.2 = (bf16[512,896]{0,1:T(8,128)(2,1)S(1)}, bf16[512,896]{0,1:T(8,128)(2,1)}, u32[]{:S(2)}) copy-start(bf16[512,896]{0,1:T(8,128)(2,1)} %copy.13) | copy-start | bytes 2752516
  196.4 10.8 %copy-start = (f32[512,896]{0,1:T(8,128)S(1)}, f32[512,896]{0,1:T(8,128)}, u32[]{:S(2)}) copy-start(f32[512,896]{0,1:T(8,128)} %convert_element_type.51) | copy-start | bytes 5505028
  196.4 10.8 %copy-start.5 = (bf16[3584,512]{1,0:T(8,128)(2,1)S(1)}, bf16[3584,512]{1,0:T(8,128)(2,1)}, u32[]{:S(2)}) copy-start(bf16[3584,512]{1,0:T(8,128)(2,1)} %all-gather.2.cloned.1.call-done) | copy-start | bytes 11010052
  206.0 1.2 copy-start.6
Sparse Core Ops, SparseCore 0:
  9.2 45.4 all-gather.1
  64.9 131.5 all-reduce.2
  213.5 133.2 all-reduce.4
where the time goes:
time: 365 us; the launch traced here: 364 us
  waiting for transfers between devices  299 us (82%)
  matrix products  35.1 us (10%)
  local copies, waits for them, and re-layouts  15.4 us (4%)
  between operations  13.2 us (4%)
    psum x2, waiting for transfers between devices, per_device(): lax.psum(partial_sum.astype(jnp.bfloat16), 'loop').astype(jnp.float32)  264 us
    all_gather x1, waiting for transfers between devices, per_device(): gathered = lax.all_gather(tokens, 'dp', axis=0, tiled=True)  34.1 us
    dot_general x2, matrix products, token_product(): lax.dot_general(token_rows, scaled_err, (((0,), (0,)), ((), ())), preferr...  18.9 us
    dot_general x2, matrix products, per_device(): partial_sum = jnp.dot(gathered, w_delta, preferred_element_type=jnp.float32)  16.2 us
  transfers between devices with their start and end apart: 3, of which 3 were waited for; matrix products, arithmetic and copies ran while one was open for 4% of the time, Pallas kernels for 0%

commit v1 on v0

--- a/solution.py
+++ b/solution.py
@@ -8,6 +8,27 @@
 step_rate = 20.0
 reg_weight = 0.05
 base_scale = 0.02
+
+
+def ring_gather(x, axis, dim):
+    size, index, rows = (lax.axis_size(axis), lax.axis_index(axis), x.shape[dim])
+    right = [(i, (i + 1) % size) for i in range(size)]
+    downward = [(i, (i - 1) % size) for i in range(size)]
+    result = jnp.zeros((*x.shape[:dim], size * rows, *x.shape[dim + 1 :]), x.dtype)
+    result = lax.dynamic_update_slice_in_dim(result, x, index * rows, axis=dim)
+    from_left = from_right = x
+    half = size // 2
+    for step in range(1, half + 1):
+        from_left = lax.ppermute(from_left, axis, right)
+        result = lax.dynamic_update_slice_in_dim(
+            result, from_left, (index - step) % size * rows, axis=dim
+        )
+        if step < size - half:
+            from_right = lax.ppermute(from_right, axis, downward)
+            result = lax.dynamic_update_slice_in_dim(
+                result, from_right, (index + step) % size * rows, axis=dim
+            )
+    return result
 
 
 def expand(block_mask):
@@ -23,7 +44,7 @@
 
 
 def per_device(tokens, weight, rounding, floor_codes, scale_codes, zero_codes, block_mask):
-    gathered = lax.all_gather(tokens, "dp", axis=0, tiled=True)
+    gathered = ring_gather(tokens, "dp", 0)
     token_count = gathered.shape[0]
     scales = base_scale * jnp.exp2(scale_codes.astype(jnp.float32) * 0.25)
     zero_point = zero_codes.astype(jnp.float32)

time: 365 us -> 383 us (1.049)
  starting transfers between devices: 0.26 us -> 34 us
  waiting for transfers between devices: 299 us -> 274 us
  local copies, waits for them, and re-layouts: 15.4 us -> 21.6 us
    all_gather x1 -> x0, waiting for transfers between devices: 34.1 us -> none  [per_device(): gathered = lax.all_gather(tokens, 'dp', axis=0, tiled=True)]
    ppermute x0 -> x15, starting transfers between devices: none -> 33.7 us  [the longest x7 32.4 us: ring_gather(): from_right = lax.ppermute(from_right, axis, downward)]
    dynamic_update_slice x0 -> x16, local copies, waits for them, and re-layouts: none -> 11.3 us  [the longest x8 5.71 us: ring_gather(): lax.dynamic_update_slice_in_dim(result, from_left, (index - step) % size...]
    ppermute x0 -> x15, waiting for transfers between devices: none -> 7 us  [the longest x8 6.58 us: ring_gather(): from_left = lax.ppermute(from_left, axis, right)]
    unnamed x17 -> x20, local copies, waits for them, and re-layouts: 7.17 us -> 1.26 us
  transfers between devices with their start and end apart: 3 -> 17, of which waited for: 3 -> 5; matrix products, arithmetic and copies ran while one was open for 4% -> 6% of each run, Pallas kernels for 0% -> 0%
where the time goes in v1:
time: 383 us
  waiting for transfers between devices  274 us (72%)
  matrix products  37.9 us (10%)
  starting transfers between devices  34 us (9%)
  local copies, waits for them, and re-layouts  21.6 us (6%)
  between operations  13.5 us (4%)
    psum x2, waiting for transfers between devices, per_device(): lax.psum(partial_sum.astype(jnp.bfloat16), 'loop').astype(jnp.float32)  267 us
    ppermute x7, starting transfers between devices, ring_gather(): from_right = lax.ppermute(from_right, axis, downward)  32.4 us
    dot_general x2, matrix products, token_product(): lax.dot_general(token_rows, scaled_err, (((0,), (0,)), ((), ())), preferr...  20 us
    dot_general x2, matrix products, per_device(): partial_sum = jnp.dot(gathered, w_delta, preferred_element_type=jnp.float32)  17.9 us
  transfers between devices with their start and end apart: 17, of which 5 were waited for; matrix products, arithmetic and copies ran while one was open for 6% of the time, Pallas kernels for 0%

profile of v1, /device:TPU:1, one launch (start us, length us, event | category | flops | bytes accessed | tf_op | source)
XLA Modules:
  0.0 383.2 jit_solution(3855963620508707117)
XLA Ops:
  6.5 3.2 collective-permute-start.1
  9.8 2.0 broadcast_in_dim.5
  11.8 0.7 constant_dynamic-update-slice_fusion.15
  12.6 2.1 broadcast_in_dim.4
  14.7 3.1 convert_element_type.45
  17.8 1.7 copy.9
  19.5 3.6 collective-permute-start.3
  23.1 0.7 constant_dynamic-update-slice_fusion.14
  25.0 4.6 %collective-permute-start.5 = (bf16[224,512]{1,0:T(8,128)(2,1)S(1)}, bf16[224,512]{1,0:T(8,128)(2,1)S(1)}, u32[]{:S(2)}, u32[]{:S(2)}) collective-permute-start(bf16[224,512]{1,0:T(8,128)(2,1)S(1)} %collective-permute-done.3), channel_id=1, source_target_pairs={{0,15},{1,0},{2,1},{3,2},{4,3},{5,4},{6,5},{7,6},{8,7},{9,8},{10,9... | collective-permute-start | bytes 688136 | tf_op jit(solution)/shard_map/ppermute | solution.py:27
  29.6 0.7 constant_dynamic-update-slice_fusion.12
  31.0 5.2 %collective-permute-start.7 = (bf16[224,512]{1,0:T(8,128)(2,1)S(1)}, bf16[224,512]{1,0:T(8,128)(2,1)S(1)}, u32[]{:S(2)}, u32[]{:S(2)}) collective-permute-start(bf16[224,512]{1,0:T(8,128)(2,1)S(1)} %collective-permute-done.5), channel_id=1, source_target_pairs={{0,15},{1,0},{2,1},{3,2},{4,3},{5,4},{6,5},{7,6},{8,7},{9,8},{10,9... | collective-permute-start | bytes 688136 | tf_op jit(solution)/shard_map/ppermute | solution.py:27
  37.7 5.2 %collective-permute-start.9 = (bf16[224,512]{1,0:T(8,128)(2,1)S(1)}, bf16[224,512]{1,0:T(8,128)(2,1)S(1)}, u32[]{:S(2)}, u32[]{:S(2)}) collective-permute-start(bf16[224,512]{1,0:T(8,128)(2,1)S(1)} %collective-permute-done.7), channel_id=1, source_target_pairs={{0,15},{1,0},{2,1},{3,2},{4,3},{5,4},{6,5},{7,6},{8,7},{9,8},{10,9... | collective-permute-start | bytes 688136 | tf_op jit(solution)/shard_map/ppermute | solution.py:27
  42.9 0.7 constant_dynamic-update-slice_fusion.8
  43.6 0.7 constant_dynamic-update-slice_fusion.7
  44.4 5.2 %collective-permute-start.11 = (bf16[224,512]{1,0:T(8,128)(2,1)S(1)}, bf16[224,512]{1,0:T(8,128)(2,1)S(1)}, u32[]{:S(2)}, u32[]{:S(2)}) collective-permute-start(bf16[224,512]{1,0:T(8,128)(2,1)S(1)} %collective-permute-done.9), channel_id=1, source_target_pairs={{0,15},{1,0},{2,1},{3,2},{4,3},{5,4},{6,5},{7,6},{8,7},{9,8},{10,9... | collective-permute-start | bytes 688136 | tf_op jit(solution)/shard_map/ppermute | solution.py:27
  49.6 0.7 constant_dynamic-update-slice_fusion.6
  50.3 0.7 constant_dynamic-update-slice_fusion.5
  51.0 5.2 %collective-permute-start.13 = (bf16[224,512]{1,0:T(8,128)(2,1)S(1)}, bf16[224,512]{1,0:T(8,128)(2,1)S(1)}, u32[]{:S(2)}, u32[]{:S(2)}) collective-permute-start(bf16[224,512]{1,0:T(8,128)(2,1)S(1)} %collective-permute-done.11), channel_id=1, source_target_pairs={{0,15},{1,0},{2,1},{3,2},{4,3},{5,4},{6,5},{7,6},{8,7},{9,8},{10,9... | collective-permute-start | bytes 688136 | tf_op jit(solution)/shard_map/ppermute | solution.py:27
  56.2 0.7 constant_dynamic-update-slice_fusion.4
  57.0 0.7 constant_dynamic-update-slice_fusion.3
  57.7 2.7 collective-permute-done.12
  60.3 1.4 collective-permute-start.14
  61.7 0.7 constant_dynamic-update-slice_fusion.2
  63.1 3.9 %collective-permute-done.14 = bf16[224,512]{1,0:T(8,128)(2,1)S(1)} collective-permute-done((bf16[224,512]{1,0:T(8,128)(2,1)S(1)}, bf16[224,512]{1,0:T(8,128)(2,1)S(1)}, u32[]{:S(2)}, u32[]{:S(2)}) %collective-permute-start.14) | collective-permute-done | bytes 229408 | tf_op jit(solution)/shard_map/ppermute | solution.py:22
  67.7 9.0 %convolution_convert_fusion.1 = bf16[3584,896]{1,0:T(8,128)(2,1)} fusion(bf16[3584,512]{1,0:T(8,128)(2,1)} %constant_dynamic-update-slice_fusion, f32[512,896]{1,0:T(8,128)S(1)} %copy-done, bf16[512,896]{1,0:T(8,128)(2,1)S(1)} %copy-done.8, s32[512,896]{1,0:T(8,128)S(1)} %copy-done.1, f32[512,896]{1,0:T(8,128)S(1)} %copy-done.7, ...), kind=kOutput, calls=%fused_computation.3 | convolution fusion | flops 3297050624 | bytes 16522240 | tf_op jit(solution)/shard_map/dot_general | solution.py:61
  76.9 1.9 compare_and_fusion
  78.8 134.0 %all-reduce.3.cloned.1.call-done = bf16[3584,896]{1,0:T(8,128)(2,1)} async-done(((bf16[3584,896]{1,0:T(8,128)(2,1)}), bf16[3584,896]{1,0:T(8,128)(2,1)}) %all-reduce.3.cloned.1.call-update) | async-done | bytes 6422544 | tf_op jit(solution)/shard_map/psum | solution.py:62
  212.8 9.5 %fusion.13 = f32[512,896]{1,0:T(8,128)S(1)} fusion(f32[512,896]{1,0:T(8,128)} %param.9, pred[512,896]{1,0:T(32,128)(4,1)S(1)} %compare_and_fusion, f32[512,896]{1,0:T(8,128)S(1)} %copy-done, bf16[3584,512]{1,0:T(8,128)(2,1)} %constant_dynamic-update-slice_fusion, bf16[3584,896]{1,0:T(8,128)(2,1)} %all-reduce.3.cloned.1.call-done, ...), kind=kOutput, calls=%fused_computation.21 | convolution fusion | flops 3305766912 | bytes 16059904 | tf_op jit(solution)/shard_map/dot_general | solution.py:41
  222.2 1.2 copy-done.9
  223.5 9.0 %convolution_convert_fusion = bf16[3584,896]{1,0:T(8,128)(2,1)} fusion(bf16[3584,512]{1,0:T(8,128)(2,1)} %constant_dynamic-update-slice_fusion, f32[512,896]{1,0:T(8,128)S(1)} %copy-done, bf16[512,896]{1,0:T(8,128)(2,1)S(1)} %copy-done.8, s32[512,896]{1,0:T(8,128)S(1)} %copy-done.2, f32[512,896]{1,0:T(8,128)S(1)} %fusion.13, ...), kind=kOutput, calls=%fused_computation.2 | convolution fusion | flops 3297050624 | bytes 16522240 | tf_op jit(solution)/shard_map/dot_general | solution.py:61
  232.4 133.4 %all-reduce.5.cloned.1.call-done = bf16[3584,896]{1,0:T(8,128)(2,1)} async-done(((bf16[3584,896]{1,0:T(8,128)(2,1)}), bf16[3584,896]{1,0:T(8,128)(2,1)}) %all-reduce.5.cloned.1.call-update) | async-done | bytes 6422544 | tf_op jit(solution)/shard_map/psum | solution.py:62
  365.8 10.6 %fusion.19 = f32[512,896]{1,0:T(8,128)} fusion(f32[512,896]{1,0:T(8,128)} %copy-done.9, pred[512,896]{1,0:T(32,128)(4,1)S(1)} %compare_and_fusion, f32[512,896]{1,0:T(8,128)S(1)} %copy-done, bf16[3584,512]{1,0:T(8,128)(2,1)} %constant_dynamic-update-slice_fusion, bf16[3584,896]{1,0:T(8,128)(2,1)} %all-reduce.5.cloned.1.call-done, ...), kind=kOutput, calls=%fused_computation.27 | convolution fusion | flops 3305766912 | bytes 16059904 | tf_op jit(solution)/shard_map/dot_general | solution.py:41
  (53 shorter events, 5.1 us)
Async XLA Ops:
  6.5 206.2 %all-reduce.3.cloned.1.call-start = ((), (), s32[]{:S(2)}) async-start(), calls=%async_computation | async-start | bytes 12845056 | tf_op jit(solution)/shard_map/psum | solution.py:62
  6.5 13.0 %collective-permute-start.1 = (bf16[224,512]{1,0:T(8,128)(2,1)}, bf16[224,512]{1,0:T(8,128)(2,1)S(1)}, u32[]{:S(2)}, u32[]{:S(2)}) collective-permute-start(bf16[224,512]{1,0:T(8,128)(2,1)} %param.7), channel_id=1, source_target_pairs={{0,15},{1,0},{2,1},{3,2},{4,3},{5,4},{6,5},{7,6},{8,7},{9,8},{10,9... | collective-permute-start | bytes 688136 | tf_op jit(solution)/shard_map/ppermute | solution.py:27
  9.7 13.4 %collective-permute-start = (bf16[224,512]{1,0:T(8,128)(2,1)}, bf16[224,512]{1,0:T(8,128)(2,1)S(1)}, u32[]{:S(2)}, u32[]{:S(2)}) collective-permute-start(bf16[224,512]{1,0:T(8,128)(2,1)} %param.7), channel_id=1, source_target_pairs={{0,1},{1,2},{2,3},{3,4},{4,5},{5,6},{6,7},{7,8},{8,9},{9,10},{10,1... | collective-permute-start | bytes 688136 | tf_op jit(solution)/shard_map/ppermute | solution.py:22
  9.7 2.0 copy-start.3
  9.7 2.7 copy-start.4
  9.7 2.7 copy-start.5
  17.8 1.7 copy-start.6
  19.5 5.5 %collective-permute-start.3 = (bf16[224,512]{1,0:T(8,128)(2,1)S(1)}, bf16[224,512]{1,0:T(8,128)(2,1)S(1)}, u32[]{:S(2)}, u32[]{:S(2)}) collective-permute-start(bf16[224,512]{1,0:T(8,128)(2,1)S(1)} %collective-permute-done.1), channel_id=1, source_target_pairs={{0,15},{1,0},{2,1},{3,2},{4,3},{5,4},{6,5},{7,6},{8,7},{9,8},{10,9... | collective-permute-start | bytes 688136 | tf_op jit(solution)/shard_map/ppermute | solution.py:27
  23.1 6.5 %collective-permute-start.2 = (bf16[224,512]{1,0:T(8,128)(2,1)S(1)}, bf16[224,512]{1,0:T(8,128)(2,1)S(1)}, u32[]{:S(2)}, u32[]{:S(2)}) collective-permute-start(bf16[224,512]{1,0:T(8,128)(2,1)S(1)} %collective-permute-done), channel_id=1, source_target_pairs={{0,1},{1,2},{2,3},{3,4},{4,5},{5,6},{6,7},{7,8},{8,9},{9,10},{10,1... | collective-permute-start | bytes 688136 | tf_op jit(solution)/shard_map/ppermute | solution.py:22
  23.9 43.8 %copy-start.8 = (bf16[512,896]{1,0:T(8,128)(2,1)S(1)}, bf16[512,896]{1,0:T(8,128)(2,1)}, u32[]{:S(2)}) copy-start(bf16[512,896]{1,0:T(8,128)(2,1)} %param.8) | copy-start | bytes 2752516
  25.0 6.0 %collective-permute-start.5 = (bf16[224,512]{1,0:T(8,128)(2,1)S(1)}, bf16[224,512]{1,0:T(8,128)(2,1)S(1)}, u32[]{:S(2)}, u32[]{:S(2)}) collective-permute-start(bf16[224,512]{1,0:T(8,128)(2,1)S(1)} %collective-permute-done.3), channel_id=1, source_target_pairs={{0,15},{1,0},{2,1},{3,2},{4,3},{5,4},{6,5},{7,6},{8,7},{9,8},{10,9... | collective-permute-start | bytes 688136 | tf_op jit(solution)/shard_map/ppermute | solution.py:27
  29.6 6.7 %collective-permute-start.4 = (bf16[224,512]{1,0:T(8,128)(2,1)S(1)}, bf16[224,512]{1,0:T(8,128)(2,1)S(1)}, u32[]{:S(2)}, u32[]{:S(2)}) collective-permute-start(bf16[224,512]{1,0:T(8,128)(2,1)S(1)} %collective-permute-done.2), channel_id=1, source_target_pairs={{0,1},{1,2},{2,3},{3,4},{4,5},{5,6},{6,7},{7,8},{8,9},{9,10},{10,1... | collective-permute-start | bytes 688136 | tf_op jit(solution)/shard_map/ppermute | solution.py:22
  30.3 37.4 %copy-start.7 = (f32[512,896]{1,0:T(8,128)S(1)}, f32[512,896]{1,0:T(8,128)}, u32[]{:S(2)}) copy-start(f32[512,896]{1,0:T(8,128)} %param.9) | copy-start | bytes 5505028
  31.0 6.7 %collective-permute-start.7 = (bf16[224,512]{1,0:T(8,128)(2,1)S(1)}, bf16[224,512]{1,0:T(8,128)(2,1)S(1)}, u32[]{:S(2)}, u32[]{:S(2)}) collective-permute-start(bf16[224,512]{1,0:T(8,128)(2,1)S(1)} %collective-permute-done.5), channel_id=1, source_target_pairs={{0,15},{1,0},{2,1},{3,2},{4,3},{5,4},{6,5},{7,6},{8,7},{9,8},{10,9... | collective-permute-start | bytes 688136 | tf_op jit(solution)/shard_map/ppermute | solution.py:27
  36.3 6.7 %collective-permute-start.6 = (bf16[224,512]{1,0:T(8,128)(2,1)S(1)}, bf16[224,512]{1,0:T(8,128)(2,1)S(1)}, u32[]{:S(2)}, u32[]{:S(2)}) collective-permute-start(bf16[224,512]{1,0:T(8,128)(2,1)S(1)} %collective-permute-done.4), channel_id=1, source_target_pairs={{0,1},{1,2},{2,3},{3,4},{4,5},{5,6},{6,7},{7,8},{8,9},{9,10},{10,1... | collective-permute-start | bytes 688136 | tf_op jit(solution)/shard_map/ppermute | solution.py:22
  37.7 6.7 %collective-permute-start.9 = (bf16[224,512]{1,0:T(8,128)(2,1)S(1)}, bf16[224,512]{1,0:T(8,128)(2,1)S(1)}, u32[]{:S(2)}, u32[]{:S(2)}) collective-permute-start(bf16[224,512]{1,0:T(8,128)(2,1)S(1)} %collective-permute-done.7), channel_id=1, source_target_pairs={{0,15},{1,0},{2,1},{3,2},{4,3},{5,4},{6,5},{7,6},{8,7},{9,8},{10,9... | collective-permute-start | bytes 688136 | tf_op jit(solution)/shard_map/ppermute | solution.py:27
  42.9 6.7 %collective-permute-start.8 = (bf16[224,512]{1,0:T(8,128)(2,1)S(1)}, bf16[224,512]{1,0:T(8,128)(2,1)S(1)}, u32[]{:S(2)}, u32[]{:S(2)}) collective-permute-start(bf16[224,512]{1,0:T(8,128)(2,1)S(1)} %collective-permute-done.6), channel_id=1, source_target_pairs={{0,1},{1,2},{2,3},{3,4},{4,5},{5,6},{6,7},{7,8},{8,9},{9,10},{10,1... | collective-permute-start | bytes 688136 | tf_op jit(solution)/shard_map/ppermute | solution.py:22
  43.6 24.1 %copy-start = (f32[512,896]{1,0:T(8,128)S(1)}, f32[512,896]{1,0:T(8,128)}, u32[]{:S(2)}) copy-start(f32[512,896]{1,0:T(8,128)} %copy.9) | copy-start | bytes 5505028
  43.6 24.1 %copy-start.1 = (s32[512,896]{1,0:T(8,128)S(1)}, s32[512,896]{1,0:T(8,128)}, u32[]{:S(2)}) copy-start(s32[512,896]{1,0:T(8,128)} %param.10) | copy-start | bytes 5505028
  44.4 6.6 %collective-permute-start.11 = (bf16[224,512]{1,0:T(8,128)(2,1)S(1)}, bf16[224,512]{1,0:T(8,128)(2,1)S(1)}, u32[]{:S(2)}, u32[]{:S(2)}) collective-permute-start(bf16[224,512]{1,0:T(8,128)(2,1)S(1)} %collective-permute-done.9), channel_id=1, source_target_pairs={{0,15},{1,0},{2,1},{3,2},{4,3},{5,4},{6,5},{7,6},{8,7},{9,8},{10,9... | collective-permute-start | bytes 688136 | tf_op jit(solution)/shard_map/ppermute | solution.py:27
  49.6 6.7 %collective-permute-start.10 = (bf16[224,512]{1,0:T(8,128)(2,1)S(1)}, bf16[224,512]{1,0:T(8,128)(2,1)S(1)}, u32[]{:S(2)}, u32[]{:S(2)}) collective-permute-start(bf16[224,512]{1,0:T(8,128)(2,1)S(1)} %collective-permute-done.8), channel_id=1, source_target_pairs={{0,1},{1,2},{2,3},{3,4},{4,5},{5,6},{6,7},{7,8},{8,9},{9,10},{10,1... | collective-permute-start | bytes 688136 | tf_op jit(solution)/shard_map/ppermute | solution.py:22
  51.0 11.4 %collective-permute-start.13 = (bf16[224,512]{1,0:T(8,128)(2,1)S(1)}, bf16[224,512]{1,0:T(8,128)(2,1)S(1)}, u32[]{:S(2)}, u32[]{:S(2)}) collective-permute-start(bf16[224,512]{1,0:T(8,128)(2,1)S(1)} %collective-permute-done.11), channel_id=1, source_target_pairs={{0,15},{1,0},{2,1},{3,2},{4,3},{5,4},{6,5},{7,6},{8,7},{9,8},{10,9... | collective-permute-start | bytes 688136 | tf_op jit(solution)/shard_map/ppermute | solution.py:27
  56.2 4.1 %collective-permute-start.12 = (bf16[224,512]{1,0:T(8,128)(2,1)S(1)}, bf16[224,512]{1,0:T(8,128)(2,1)S(1)}, u32[]{:S(2)}, u32[]{:S(2)}) collective-permute-start(bf16[224,512]{1,0:T(8,128)(2,1)S(1)} %collective-permute-done.10), channel_id=1, source_target_pairs={{0,1},{1,2},{2,3},{3,4},{4,5},{5,6},{6,7},{7,8},{8,9},{9,10},{10,1... | collective-permute-start | bytes 688136 | tf_op jit(solution)/shard_map/ppermute | solution.py:22
  60.3 6.7 %collective-permute-start.14 = (bf16[224,512]{1,0:T(8,128)(2,1)S(1)}, bf16[224,512]{1,0:T(8,128)(2,1)S(1)}, u32[]{:S(2)}, u32[]{:S(2)}) collective-permute-start(bf16[224,512]{1,0:T(8,128)(2,1)S(1)} %collective-permute-done.12), channel_id=1, source_target_pairs={{0,1},{1,2},{2,3},{3,4},{4,5},{5,6},{6,7},{7,8},{8,9},{9,10},{10,1... | collective-permute-start | bytes 688136 | tf_op jit(solution)/shard_map/ppermute | solution.py:22
  76.7 289.1 %all-reduce.5.cloned.1.call-start = ((), (), s32[]{:S(2)}) async-start(), calls=%async_computation.1 | async-start | bytes 12845056 | tf_op jit(solution)/shard_map/psum | solution.py:62
  212.8 10.7 %copy-start.2 = (s32[512,896]{1,0:T(8,128)S(1)}, s32[512,896]{1,0:T(8,128)}, u32[]{:S(2)}) copy-start(s32[512,896]{1,0:T(8,128)} %param.10) | copy-start | bytes 5505028
  222.2 1.2 copy-start.9
Sparse Core Ops, SparseCore 0:
  76.8 135.9 all-reduce.2
  232.6 133.2 all-reduce.4
